TPU v7x, 1024 devices: a whole 4x4x32 slice. The times are simulated.
1024 devices in a mesh: seq: 64 (over z, core), chan: 16 (over y, x).
Axes of the slice: x: 4, y: 4, z: 32, core: 2. Of those that a mesh axis runs over, the one named last changes fastest.
Arguments:
- mixer_input: bfloat16 [8192, 2048], P('seq', 'chan'), may hold values from -6 to 6
- gate_branch: bfloat16 [8192, 2048], P('seq', 'chan'), may hold values from -6 to 6
- skip_gain: float32 [2048], P('chan'), may hold values from -3 to 3
- decay_rate: float32 [2048], P('chan'), may hold values from 0.1 to 512
- first_weight: float32 [33, 64], replicated, may hold values from -1 to 1
- first_bias: float32 [64], replicated, may hold values from -4 to 4
- second_weight: float32 [64, 64], replicated, may hold values from -0.75 to 0.75
- second_bias: float32 [64], replicated, may hold values from -4 to 4
- last_weight: float32 [64, 2048], P(None, 'chan'), may hold values from -0.75 to 0.75
- output_weight: bfloat16 [2048, 4096], P('chan'), may hold values from -0.1875 to 0.1875
Outputs:
- projected: bfloat16 [8192, 4096], P('seq', 'chan')
All inputs are finite; a program needn't handle non-finite values.
Results may differ from a plain program's by a relative error of at most 0.0049.
Values may be sent and summed in bfloat16 or wider, within the bound.
A program may use at most 32 MiB of HBM per device.

v0:
```python
import functools
import math

import jax
import jax.numpy as jnp
import ml_dtypes
import numpy as np
from jax import lax
from jax.experimental import pallas as pl
from jax.experimental.pallas import tpu as pltpu
from jax.sharding import PartitionSpec as P

HIGHEST = lax.Precision.HIGHEST
F32 = jnp.float32
BF16 = jnp.bfloat16
MESH = pl.DeviceIdType.MESH


def band_frequencies(length, emb_width):
    band_count = (emb_width - 1) // 2
    return [
        min(length // 2, max(b, int((length / 2) ** ((b - 1) / (band_count - 1)))))
        for b in range(1, band_count + 1)
    ]


def two_terms(table):
    high = table.astype(np.float32).astype(ml_dtypes.bfloat16)
    low = (table - high.astype(np.float64)).astype(np.float32).astype(ml_dtypes.bfloat16)
    return high, low


def transform_tables(blocks, width):
    length = blocks * width
    k1 = np.arange(blocks)[:, None]
    b = np.arange(blocks)[None, :]
    across = 2.0 * math.pi * (k1 + 0.25) * b / blocks
    first = np.concatenate([np.cos(across), -np.sin(across)], axis=0)
    last = np.concatenate([np.cos(across).T, -np.sin(across).T], axis=1) / length
    j = np.arange(width)
    turn = 2.0 * math.pi * (k1 + 0.25) * j[None, :] / length
    twiddle = np.stack([np.cos(turn), np.sin(turn)]).astype(np.float32)
    within = 2.0 * math.pi * ((j[:, None] * j[None, :]) % width) / width
    cos, sin = np.cos(within), np.sin(within)
    middle = np.block([[cos, -sin], [sin, cos]])
    return (
        *two_terms(first),
        twiddle,
        *two_terms(middle),
        *two_terms(middle.T),
        *two_terms(last),
    )


def split(value):
    high = value.astype(BF16)
    return high, (value - high.astype(F32)).astype(BF16)


def dot(left, right):
    return jnp.dot(left, right, preferred_element_type=F32)


def dot_terms(left, right):
    (left_high, left_low), (right_high, right_low) = left, right
    return dot(left_high, right_high) + (dot(left_low, right_high) + dot(left_high, right_low))


def contract_first(left, right):
    return lax.dot_general(
        left, right, (((0,), (0,)), ((), ())), precision=HIGHEST, preferred_element_type=F32
    )


def taps_block(
    start, length, freqs, width, w1_ref, b1_ref, w2_ref, b2_ref, wl_ref, decay_ref, pad1, pad2, hid
):
    emb, order = w1_ref.shape
    rows = pad1.shape[0]
    row = lax.broadcasted_iota(jnp.int32, (rows, width), 0)
    time = start + lax.broadcasted_iota(jnp.int32, (rows, width), 1)
    freq = jnp.zeros((rows, width), jnp.int32)
    for band, f in enumerate(freqs):
        freq = jnp.where((row == 2 * band + 1) | (row == 2 * band + 2), f, freq)
    shift = jnp.where(lax.rem(row, 2) == 1, length // 4, 0)
    phase = lax.rem(time * freq + shift, length).astype(F32) * (2.0 * math.pi / length)
    features = jnp.where(row == 0, time.astype(F32) / length, jnp.sin(phase))
    features = jnp.where(row == emb, 1.0, jnp.where(row > emb, 0.0, features))
    pad1[...] = jnp.zeros_like(pad1)
    pad1[0:emb, :] = w1_ref[...]
    pad1[emb : emb + 1, :] = b1_ref[...]
    hid[0:order, :] = jnp.sin(contract_first(pad1[...], features))
    extra = lax.broadcasted_iota(jnp.int32, (hid.shape[0] - order, width), 0)
    hid[order:, :] = jnp.where(extra == 0, 1.0, 0.0)
    pad2[...] = jnp.zeros_like(pad2)
    pad2[0:order, :] = w2_ref[...]
    pad2[order : order + 1, :] = b2_ref[...]
    hidden_two = jnp.sin(contract_first(pad2[...], hid[...]))
    shaped = contract_first(wl_ref[...], hidden_two)
    chans = shaped.shape[0]
    rate = decay_ref[...]
    small = rate * (-2.0 / length)
    series = jnp.ones_like(small)
    for term in range(8, 1, -1):
        series = 1.0 + series * small * (1.0 / term)
    scale = lax.rsqrt((jnp.exp(-2.0 * rate) - 1.0) / (small * series))
    rates = jnp.broadcast_to(rate, (width, chans)).T
    scales = jnp.broadcast_to(scale, (width, chans)).T
    fraction = (start + lax.broadcasted_iota(jnp.int32, (chans, width), 1)).astype(F32) / length
    return shaped * jnp.exp(-rates * fraction) * scales


def convolve(per, recv, send, lhs, mid, first, twiddle, forward, backward, last):
    blocks, _, width = recv.shape
    both = 2 * per
    first_high, first_low = first
    source = jnp.concatenate([recv[:, i, :] for i in range(both)], axis=1)
    high, low = split(source)
    stage = dot(first_high, high) + (dot(first_low, high) + dot(first_high, low))
    cos, sin = twiddle[0], twiddle[1]
    for i in range(both):
        re = stage[:blocks, i * width : (i + 1) * width]
        im = stage[blocks:, i * width : (i + 1) * width]
        lhs[i * blocks : (i + 1) * blocks, :width] = re * cos + im * sin
        lhs[i * blocks : (i + 1) * blocks, width:] = im * cos - re * sin
    spectrum = dot_terms(split(lhs[...]), (forward[0][...], forward[1][...]))
    half = per * blocks
    x_re, x_im = spectrum[:half, :width], spectrum[:half, width:]
    h_re, h_im = spectrum[half:, :width], spectrum[half:, width:]
    lhs[:half, :width] = x_re * h_re - x_im * h_im
    lhs[:half, width:] = x_re * h_im + x_im * h_re
    stage = dot_terms(split(lhs[:half, :]), (backward[0][...], backward[1][...]))
    for i in range(per):
        re = stage[i * blocks : (i + 1) * blocks, :width]
        im = stage[i * blocks : (i + 1) * blocks, width:]
        mid[:blocks, i * width : (i + 1) * width] = re * cos - im * sin
        mid[blocks:, i * width : (i + 1) * width] = re * sin + im * cos
    result = dot_terms(last, split(mid[...]))
    for i in range(per):
        send[:, i, :] = result[:, i * width : (i + 1) * width]


def mixer_kernel(
    seq_size,
    chan_size,
    freqs,
    x_ref,
    gate_ref,
    skip_ref,
    decay_ref,
    w1_ref,
    b1_ref,
    w2_ref,
    b2_ref,
    wl_ref,
    first_high,
    first_low,
    twiddle,
    forward_high,
    forward_low,
    backward_high,
    backward_low,
    last_high,
    last_low,
    weight_hbm,
    out_ref,
    pad1,
    pad2,
    hid,
    send1,
    recv1,
    lhs,
    mid,
    send2,
    recv2,
    mixed,
    gathered,
    columns,
    send_sems,
    recv_sems,
    local_sem,
):
    block, chans = x_ref.shape
    per = chans // seq_size
    feats = out_ref.shape[1]
    d = lax.axis_index("seq")
    c = lax.axis_index("chan")

    def seq_peer(k):
        return lax.rem(d + k, seq_size)

    def chan_peer(k):
        return lax.rem(c + k, chan_size)

    barrier = pltpu.get_barrier_semaphore()

    @pl.loop(1, seq_size)
    def _(k):
        pl.semaphore_signal(
            barrier, inc=1, device_id={"seq": seq_peer(k)}, device_id_type=MESH
        )

    @pl.loop(1, chan_size)
    def _(k):
        pl.semaphore_signal(
            barrier, inc=1, device_id={"chan": chan_peer(k)}, device_id_type=MESH
        )

    own_columns = pltpu.make_async_copy(
        weight_hbm.at[:, pl.ds(pl.multiple_of(c * feats, feats), feats)],
        columns.at[pl.ds(pl.multiple_of(c * chans, chans), chans), :],
        local_sem,
    )
    own_columns.start()

    taps = taps_block(
        d * block,
        seq_size * block,
        freqs,
        block,
        w1_ref,
        b1_ref,
        w2_ref,
        b2_ref,
        wl_ref,
        decay_ref,
        pad1,
        pad2,
        hid,
    )
    turned = x_ref[...].astype(F32).T
    for i in range(per):
        send1[:, i, :] = turned[i * seq_size : (i + 1) * seq_size, :]
        send1[:, per + i, :] = taps[i * seq_size : (i + 1) * seq_size, :]

    pl.semaphore_wait(barrier, seq_size - 1 + chan_size - 1)

    @pl.loop(1, seq_size)
    def _(k):
        p = seq_peer(k)
        pltpu.make_async_remote_copy(
            src_ref=send1.at[p],
            dst_ref=recv1.at[d],
            send_sem=send_sems.at[0],
            recv_sem=recv_sems.at[0],
            device_id={"seq": p},
            device_id_type=MESH,
        ).start()

    @pl.loop(1, chan_size)
    def _(k):
        p = chan_peer(k)
        pltpu.make_async_remote_copy(
            src_ref=weight_hbm.at[:, pl.ds(pl.multiple_of(p * feats, feats), feats)],
            dst_ref=columns.at[pl.ds(pl.multiple_of(c * chans, chans), chans), :],
            send_sem=send_sems.at[1],
            recv_sem=recv_sems.at[1],
            device_id={"chan": p},
            device_id_type=MESH,
        ).start()

    recv1[d] = send1[d]

    def wait_bytes(ref, sem):
        pltpu.make_async_copy(ref, ref, sem).wait()

    others = pl.ds(0, seq_size - 1)
    wait_bytes(recv1.at[others], recv_sems.at[0])

    convolve(
        per,
        recv1,
        send2,
        lhs,
        mid,
        (first_high[...], first_low[...]),
        twiddle,
        (forward_high, forward_low),
        (backward_high, backward_low),
        (last_high[...], last_low[...]),
    )

    @pl.loop(1, seq_size)
    def _(k):
        p = seq_peer(k)
        pltpu.make_async_remote_copy(
            src_ref=send2.at[p],
            dst_ref=recv2.at[d],
            send_sem=send_sems.at[2],
            recv_sem=recv_sems.at[2],
            device_id={"seq": p},
            device_id_type=MESH,
        ).start()

    recv2[d] = send2[d]
    skipped = skip_ref[...] * x_ref[...].astype(F32)
    gate = gate_ref[...].astype(F32)
    wait_bytes(recv2.at[others], recv_sems.at[2])
    convolved = jnp.concatenate([recv2[:, i, :] for i in range(per)], axis=0).T
    mixed[...] = (gate * (convolved + skipped)).astype(BF16)

    here = gathered.at[:, pl.ds(pl.multiple_of(c * chans, chans), chans)]

    @pl.loop(1, chan_size)
    def _(k):
        pltpu.make_async_remote_copy(
            src_ref=mixed,
            dst_ref=here,
            send_sem=send_sems.at[3],
            recv_sem=recv_sems.at[3],
            device_id={"chan": chan_peer(k)},
            device_id_type=MESH,
        ).start()

    here[...] = mixed[...]
    own_columns.wait()
    rest = pl.ds(0, (chan_size - 1) * chans)
    wait_bytes(columns.at[rest, :], recv_sems.at[1])
    wait_bytes(gathered.at[:, rest], recv_sems.at[3])
    out_ref[...] = dot(gathered[...], columns[...]).astype(out_ref.dtype)

    wait_bytes(send1.at[others], send_sems.at[0])
    wait_bytes(columns.at[rest, :], send_sems.at[1])
    wait_bytes(send2.at[others], send_sems.at[2])
    wait_bytes(gathered.at[:, rest], send_sems.at[3])


def shards(
    mixer_input,
    gate_branch,
    skip_gain,
    decay_rate,
    first_weight,
    first_bias,
    second_weight,
    second_bias,
    last_weight,
    output_weight,
):
    block, chans = mixer_input.shape
    seq_size = lax.axis_size("seq")
    chan_size = lax.axis_size("chan")
    emb, order = first_weight.shape
    feats = output_weight.shape[1] // chan_size
    per = chans // seq_size
    length = block * seq_size
    tables = transform_tables(seq_size, block)
    vmem = pl.BlockSpec(memory_space=pltpu.VMEM)
    return pl.pallas_call(
        functools.partial(mixer_kernel, seq_size, chan_size, band_frequencies(length, emb)),
        out_shape=jax.ShapeDtypeStruct((block, feats), BF16),
        in_specs=[vmem] * (9 + len(tables)) + [pl.BlockSpec(memory_space=pl.ANY)],
        out_specs=vmem,
        scratch_shapes=[
            pltpu.VMEM((-(-(emb + 1) // 8) * 8, order), F32),
            pltpu.VMEM((order + 8, order), F32),
            pltpu.VMEM((order + 8, block), F32),
            pltpu.VMEM((seq_size, 2 * per, block), F32),
            pltpu.VMEM((seq_size, 2 * per, block), F32),
            pltpu.VMEM((2 * chans, 2 * block), F32),
            pltpu.VMEM((2 * seq_size, per * block), F32),
            pltpu.VMEM((seq_size, per, block), F32),
            pltpu.VMEM((seq_size, per, block), F32),
            pltpu.VMEM((block, chans), BF16),
            pltpu.VMEM((block, chan_size * chans), BF16),
            pltpu.VMEM((chan_size * chans, feats), BF16),
            pltpu.SemaphoreType.DMA((4,)),
            pltpu.SemaphoreType.DMA((4,)),
            pltpu.SemaphoreType.DMA,
        ],
        compiler_params=pltpu.CompilerParams(
            collective_id=0, has_side_effects=True, vmem_limit_bytes=32 << 20
        ),
    )(
        mixer_input,
        gate_branch,
        skip_gain.reshape(1, chans),
        decay_rate.reshape(1, chans),
        first_weight,
        first_bias.reshape(1, order),
        second_weight,
        second_bias.reshape(1, order),
        last_weight,
        *[jnp.asarray(table) for table in tables],
        output_weight,
    )


def solution(mesh):
    in_specs = (
        P("seq", "chan"),
        P("seq", "chan"),
        P("chan"),
        P("chan"),
        P(),
        P(),
        P(),
        P(),
        P(None, "chan"),
        P("chan", None),
    )
    out_specs = P("seq", "chan")
    return jax.shard_map(shards, mesh=mesh, in_specs=in_specs, out_specs=out_specs, check_vma=False)
```

profile of v0, /device:TPU:1, one launch (start us, length us, event | category | flops | bytes accessed | tf_op | source)
XLA Modules:
  0.0 88.8 jit_solution(2886328940824619544)
XLA Ops:
  0.0 0.0 copy-start.13
  0.0 0.0 copy-start.18
  0.0 0.0 copy-start.15
  0.0 0.0 copy-start.16
  0.0 0.0 copy-start.17
  0.0 0.7 copy-done.13
  0.7 0.0 copy-done.18
  0.7 0.0 copy-done.15
  0.7 0.0 copy-done.16
  0.7 0.0 copy-done.17
  0.7 0.0 copy-start
  0.7 1.2 %copy-done = bf16[128,4096]{1,0:T(8,128)(2,1)S(1)} copy-done((bf16[128,4096]{1,0:T(8,128)(2,1)S(1)}, bf16[128,4096]{1,0:T(8,128)(2,1)}, u32[]{:S(2)}) %copy-start) | copy-done | bytes 1048600
  2.0 0.0 copy-start.1
  2.0 0.9 %copy-done.1 = bf16[256,256]{1,0:T(8,128)(2,1)S(1)} copy-done((bf16[256,256]{1,0:T(8,128)(2,1)S(1)}, bf16[256,256]{1,0:T(8,128)(2,1)}, u32[]{:S(2)}) %copy-start.1) | copy-done | bytes 131096
  2.9 0.0 copy-start.2
  2.9 0.9 %copy-done.2 = bf16[256,256]{1,0:T(8,128)(2,1)S(1)} copy-done((bf16[256,256]{1,0:T(8,128)(2,1)S(1)}, bf16[256,256]{1,0:T(8,128)(2,1)}, u32[]{:S(2)}) %copy-start.2) | copy-done | bytes 131096
  3.8 0.0 copy-start.3
  3.8 0.9 %copy-done.3 = bf16[256,256]{1,0:T(8,128)(2,1)S(1)} copy-done((bf16[256,256]{1,0:T(8,128)(2,1)S(1)}, bf16[256,256]{1,0:T(8,128)(2,1)}, u32[]{:S(2)}) %copy-start.3) | copy-done | bytes 131096
  4.7 0.0 copy-start.4
  4.7 0.9 %copy-done.4 = bf16[256,256]{1,0:T(8,128)(2,1)S(1)} copy-done((bf16[256,256]{1,0:T(8,128)(2,1)S(1)}, bf16[256,256]{1,0:T(8,128)(2,1)}, u32[]{:S(2)}) %copy-start.4) | copy-done | bytes 131096
  5.6 0.0 copy-start.5
  5.6 0.8 copy-done.5
  6.4 0.0 copy-start.6
  6.4 0.8 copy-done.6
  7.2 0.0 copy-start.7
  7.2 0.8 copy-done.7
  7.9 0.0 copy-start.8
  7.9 0.8 copy-done.8
  8.7 0.0 copy-start.9
  8.7 0.8 copy-done.9
  9.5 0.0 copy-start.10
  9.5 0.8 copy-done.10
  10.2 0.0 copy-start.11
  10.2 0.8 copy-done.11
  11.0 0.0 copy-start.12
  11.0 0.7 copy-done.12
  11.7 0.0 copy-start.14
  11.7 0.7 copy-done.14
  12.4 75.8 %shard_map.181 = bf16[128,256]{1,0:T(8,128)(2,1)S(1)} custom-call(bf16[128,128]{1,0:T(8,128)(2,1)S(1)} %copy-done.6, bf16[128,128]{1,0:T(8,128)(2,1)S(1)} %copy-done.7, f32[1,128]{1,0:T(1,128)S(1)} %bitcast.4, f32[1,128]{1,0:T(1,128)S(1)} %bitcast.5, f32[33,64]{1,0:T(8,128)S(1)} %copy-done.12, f32[1,64]{1,0:T(1,128)S(1)} %bitcast.6, f32[64,64]{1,0:T(8,128)S(1)} %copy-done.8, ...), custom_call_target="tpu_custom_call" | custom-call | tf_op jit(solution)/shard_map/pallas_call | solution.py:349
  88.2 0.6 copy.21
Async XLA Ops:
  0.0 0.7 copy-start.13
  0.0 0.7 copy-start.18
  0.0 0.7 copy-start.15
  0.0 0.7 copy-start.16
  0.0 0.7 copy-start.17
  0.7 1.2 %copy-start = (bf16[128,4096]{1,0:T(8,128)(2,1)S(1)}, bf16[128,4096]{1,0:T(8,128)(2,1)}, u32[]{:S(2)}) copy-start(bf16[128,4096]{1,0:T(8,128)(2,1)} %weight_hbm.1) | copy-start | bytes 3145732
  2.0 0.9 %copy-start.1 = (bf16[256,256]{1,0:T(8,128)(2,1)S(1)}, bf16[256,256]{1,0:T(8,128)(2,1)}, u32[]{:S(2)}) copy-start(bf16[256,256]{1,0:T(8,128)(2,1)} %constant.24.clone.backward_low) | copy-start | bytes 393220
  2.9 0.9 %copy-start.2 = (bf16[256,256]{1,0:T(8,128)(2,1)S(1)}, bf16[256,256]{1,0:T(8,128)(2,1)}, u32[]{:S(2)}) copy-start(bf16[256,256]{1,0:T(8,128)(2,1)} %constant.23.clone.backward_high) | copy-start | bytes 393220
  3.8 0.9 %copy-start.3 = (bf16[256,256]{1,0:T(8,128)(2,1)S(1)}, bf16[256,256]{1,0:T(8,128)(2,1)}, u32[]{:S(2)}) copy-start(bf16[256,256]{1,0:T(8,128)(2,1)} %constant.22.clone.forward_low) | copy-start | bytes 393220
  4.7 0.9 %copy-start.4 = (bf16[256,256]{1,0:T(8,128)(2,1)S(1)}, bf16[256,256]{1,0:T(8,128)(2,1)}, u32[]{:S(2)}) copy-start(bf16[256,256]{1,0:T(8,128)(2,1)} %constant.21.clone.forward_high) | copy-start | bytes 393220
  5.6 0.8 copy-start.5
  6.4 0.8 copy-start.6
  7.2 0.8 copy-start.7
  7.9 0.8 copy-start.8
  8.7 0.8 copy-start.9
  9.5 0.8 copy-start.10
  10.2 0.8 copy-start.11
  11.0 0.7 copy-start.12
  11.7 0.7 copy-start.14
where the time goes:
time: 89.7 us; the launch traced here: 88.8 us
  Pallas kernels  75.8 us (85%)
  local copies, waits for them, and re-layouts  13 us (14%)
    pallas_call x1, Pallas kernels, shards(): pl.pallas_call(functools.partial(mixer_kernel, seq_size, chan_size, band_...  75.8 us
    unnamed x39, local copies, waits for them, and re-layouts  13 us

commit v1 on v0

--- a/solution.py
+++ b/solution.py
@@ -39,17 +39,14 @@
     last = np.concatenate([np.cos(across).T, -np.sin(across).T], axis=1) / length
     j = np.arange(width)
     turn = 2.0 * math.pi * (k1 + 0.25) * j[None, :] / length
-    twiddle = np.stack([np.cos(turn), np.sin(turn)]).astype(np.float32)
+    twiddle = np.concatenate([np.cos(turn), np.sin(turn)]).astype(np.float32)
     within = 2.0 * math.pi * ((j[:, None] * j[None, :]) % width) / width
     cos, sin = np.cos(within), np.sin(within)
-    middle = np.block([[cos, -sin], [sin, cos]])
-    return (
-        *two_terms(first),
-        twiddle,
-        *two_terms(middle),
-        *two_terms(middle.T),
-        *two_terms(last),
-    )
+    middle = np.concatenate(two_terms(np.block([[cos, -sin], [sin, cos]])), axis=0)
+    first_high, first_low = two_terms(first)
+    first = np.concatenate([first_high, first_low, first_high, first_low], axis=1)
+    last = np.concatenate(two_terms(last), axis=1)
+    return twiddle, middle, first, last
 
 
 def split(value):
@@ -61,9 +58,8 @@
     return jnp.dot(left, right, preferred_element_type=F32)
 
 
-def dot_terms(left, right):
-    (left_high, left_low), (right_high, right_low) = left, right
-    return dot(left_high, right_high) + (dot(left_low, right_high) + dot(left_high, right_low))
+def dot_nt(left, right):
+    return lax.dot_general(left, right, (((1,), (1,)), ((), ())), preferred_element_type=F32)
 
 
 def contract_first(left, right):
@@ -110,76 +106,60 @@
     return shaped * jnp.exp(-rates * fraction) * scales
 
 
-def convolve(per, recv, send, lhs, mid, first, twiddle, forward, backward, last):
+def convolve(per, recv, send, lhs, mid, twiddle, middle, first, last):
     blocks, _, width = recv.shape
     both = 2 * per
-    first_high, first_low = first
-    source = jnp.concatenate([recv[:, i, :] for i in range(both)], axis=1)
-    high, low = split(source)
-    stage = dot(first_high, high) + (dot(first_low, high) + dot(first_high, low))
-    cos, sin = twiddle[0], twiddle[1]
+    high, low = split(jnp.concatenate([recv[:, i, :] for i in range(both)], axis=1))
+    stage = dot(first[...], jnp.concatenate([high, high, low, low], axis=0))
+    cos, sin = twiddle[:blocks, :], twiddle[blocks:, :]
     for i in range(both):
         re = stage[:blocks, i * width : (i + 1) * width]
         im = stage[blocks:, i * width : (i + 1) * width]
         lhs[i * blocks : (i + 1) * blocks, :width] = re * cos + im * sin
         lhs[i * blocks : (i + 1) * blocks, width:] = im * cos - re * sin
-    spectrum = dot_terms(split(lhs[...]), (forward[0][...], forward[1][...]))
+    table_high, table_low = middle[: 2 * width, :], middle[2 * width :, :]
+    high, low = split(lhs[...])
+    spectrum = dot(high, table_high) + (dot(low, table_high) + dot(high, table_low))
     half = per * blocks
     x_re, x_im = spectrum[:half, :width], spectrum[:half, width:]
     h_re, h_im = spectrum[half:, :width], spectrum[half:, width:]
-    lhs[:half, :width] = x_re * h_re - x_im * h_im
-    lhs[:half, width:] = x_re * h_im + x_im * h_re
-    stage = dot_terms(split(lhs[:half, :]), (backward[0][...], backward[1][...]))
+    product = jnp.concatenate([x_re * h_re - x_im * h_im, x_re * h_im + x_im * h_re], axis=1)
+    high, low = split(product)
+    stage = dot_nt(high, table_high) + (dot_nt(low, table_high) + dot_nt(high, table_low))
     for i in range(per):
         re = stage[i * blocks : (i + 1) * blocks, :width]
         im = stage[i * blocks : (i + 1) * blocks, width:]
         mid[:blocks, i * width : (i + 1) * width] = re * cos - im * sin
         mid[blocks:, i * width : (i + 1) * width] = re * sin + im * cos
-    result = dot_terms(last, split(mid[...]))
+    high, low = split(mid[...])
+    table = last[...]
+    result = dot(table, jnp.concatenate([high, high], axis=0))
+    result += dot(table, jnp.concatenate([low, low], axis=0))
     for i in range(per):
         send[:, i, :] = result[:, i * width : (i + 1) * width]
 
 
-def mixer_kernel(
-    seq_size,
-    chan_size,
-    freqs,
-    x_ref,
-    gate_ref,
-    skip_ref,
-    decay_ref,
-    w1_ref,
-    b1_ref,
-    w2_ref,
-    b2_ref,
-    wl_ref,
-    first_high,
-    first_low,
-    twiddle,
-    forward_high,
-    forward_low,
-    backward_high,
-    backward_low,
-    last_high,
-    last_low,
-    weight_hbm,
-    out_ref,
-    pad1,
-    pad2,
-    hid,
-    send1,
-    recv1,
-    lhs,
-    mid,
-    send2,
-    recv2,
-    mixed,
-    gathered,
-    columns,
-    send_sems,
-    recv_sems,
-    local_sem,
-):
+def mixer_kernel(seq_size, chan_size, freqs, arrays, *refs):
+    sources, weight_hbm, out_ref = refs[:arrays], refs[arrays], refs[arrays + 1]
+    held = refs[arrays + 2 : 2 * arrays + 2]
+    x_ref, gate_ref, skip_ref, decay_ref, w1_ref, b1_ref, w2_ref, b2_ref, wl_ref = held[:9]
+    (
+        pad1,
+        pad2,
+        hid,
+        send1,
+        recv1,
+        lhs,
+        mid,
+        send2,
+        recv2,
+        mixed,
+        gathered,
+        columns,
+        send_sems,
+        recv_sems,
+        local_sems,
+    ) = refs[2 * arrays + 2 :]
     block, chans = x_ref.shape
     per = chans // seq_size
     feats = out_ref.shape[1]
@@ -192,6 +172,12 @@
     def chan_peer(k):
         return lax.rem(c + k, chan_size)
 
+    loads = [
+        pltpu.make_async_copy(source, target, local_sems.at[i])
+        for i, (source, target) in enumerate(zip(sources, held))
+    ]
+    for load in loads:
+        load.start()
     barrier = pltpu.get_barrier_semaphore()
 
     @pl.loop(1, seq_size)
@@ -209,9 +195,11 @@
     own_columns = pltpu.make_async_copy(
         weight_hbm.at[:, pl.ds(pl.multiple_of(c * feats, feats), feats)],
         columns.at[pl.ds(pl.multiple_of(c * chans, chans), chans), :],
-        local_sem,
+        local_sems.at[arrays],
     )
     own_columns.start()
+    for load in loads:
+        load.wait()
 
     taps = taps_block(
         d * block,
@@ -235,6 +223,12 @@
 
     pl.semaphore_wait(barrier, seq_size - 1 + chan_size - 1)
 
+    def wait_bytes(ref, sem):
+        pltpu.make_async_copy(ref, ref, sem).wait()
+
+    others = pl.ds(0, seq_size - 1)
+    rest = pl.ds(0, (chan_size - 1) * chans)
+
     @pl.loop(1, seq_size)
     def _(k):
         p = seq_peer(k)
@@ -247,6 +241,7 @@
             device_id_type=MESH,
         ).start()
 
+
     @pl.loop(1, chan_size)
     def _(k):
         p = chan_peer(k)
@@ -261,24 +256,10 @@
 
     recv1[d] = send1[d]
 
-    def wait_bytes(ref, sem):
-        pltpu.make_async_copy(ref, ref, sem).wait()
-
-    others = pl.ds(0, seq_size - 1)
     wait_bytes(recv1.at[others], recv_sems.at[0])
 
-    convolve(
-        per,
-        recv1,
-        send2,
-        lhs,
-        mid,
-        (first_high[...], first_low[...]),
-        twiddle,
-        (forward_high, forward_low),
-        (backward_high, backward_low),
-        (last_high[...], last_low[...]),
-    )
+    convolve(per, recv1, send2, lhs, mid, *held[9:])
+
 
     @pl.loop(1, seq_size)
     def _(k):
@@ -314,7 +295,6 @@
 
     here[...] = mixed[...]
     own_columns.wait()
-    rest = pl.ds(0, (chan_size - 1) * chans)
     wait_bytes(columns.at[rest, :], recv_sems.at[1])
     wait_bytes(gathered.at[:, rest], recv_sems.at[3])
     out_ref[...] = dot(gathered[...], columns[...]).astype(out_ref.dtype)
@@ -344,14 +324,27 @@
     feats = output_weight.shape[1] // chan_size
     per = chans // seq_size
     length = block * seq_size
-    tables = transform_tables(seq_size, block)
-    vmem = pl.BlockSpec(memory_space=pltpu.VMEM)
+    held = [
+        mixer_input,
+        gate_branch,
+        skip_gain.reshape(1, chans),
+        decay_rate.reshape(1, chans),
+        first_weight,
+        first_bias.reshape(1, order),
+        second_weight,
+        second_bias.reshape(1, order),
+        last_weight,
+        *[jnp.asarray(table) for table in transform_tables(seq_size, block)],
+    ]
     return pl.pallas_call(
-        functools.partial(mixer_kernel, seq_size, chan_size, band_frequencies(length, emb)),
+        functools.partial(
+            mixer_kernel, seq_size, chan_size, band_frequencies(length, emb), len(held)
+        ),
         out_shape=jax.ShapeDtypeStruct((block, feats), BF16),
-        in_specs=[vmem] * (9 + len(tables)) + [pl.BlockSpec(memory_space=pl.ANY)],
-        out_specs=vmem,
+        in_specs=[pl.BlockSpec(memory_space=pltpu.HBM)] * (len(held) + 1),
+        out_specs=pl.BlockSpec(memory_space=pltpu.VMEM),
         scratch_shapes=[
+            *[pltpu.VMEM(value.shape, value.dtype) for value in held],
             pltpu.VMEM((-(-(emb + 1) // 8) * 8, order), F32),
             pltpu.VMEM((order + 8, order), F32),
             pltpu.VMEM((order + 8, block), F32),
@@ -366,24 +359,12 @@
             pltpu.VMEM((chan_size * chans, feats), BF16),
             pltpu.SemaphoreType.DMA((4,)),
             pltpu.SemaphoreType.DMA((4,)),
-            pltpu.SemaphoreType.DMA,
+            pltpu.SemaphoreType.DMA((len(held) + 1,)),
         ],
         compiler_params=pltpu.CompilerParams(
-            collective_id=0, has_side_effects=True, vmem_limit_bytes=32 << 20
+            collective_id=0, has_side_effects=True, vmem_limit_bytes=62 << 20
         ),
-    )(
-        mixer_input,
-        gate_branch,
-        skip_gain.reshape(1, chans),
-        decay_rate.reshape(1, chans),
-        first_weight,
-        first_bias.reshape(1, order),
-        second_weight,
-        second_bias.reshape(1, order),
-        last_weight,
-        *[jnp.asarray(table) for table in tables],
-        output_weight,
-    )
+    )(*held, output_weight)
 
 
 def solution(mesh):

time: 89.7 us -> 78 us (0.87)
  local copies, waits for them, and re-layouts: 13 us -> 1.47 us
    unnamed x39 -> x1, local copies, waits for them, and re-layouts: 13 us -> 1.47 us
where the time goes in v1:
time: 78 us; the launch traced here: 77.8 us
  Pallas kernels  76.3 us (98%)
  local copies, waits for them, and re-layouts  1.47 us (2%)
    pallas_call x1, Pallas kernels, shards(): pl.pallas_call(functools.partial(mixer_kernel, seq_size, chan_size, band_...  76.3 us

profile of v1, /device:TPU:1, one launch (start us, length us, event | category | flops | bytes accessed | tf_op | source)
XLA Modules:
  0.0 77.8 jit_solution(10336374713761914027)
XLA Ops:
  0.0 76.3 %shard_map.136 = bf16[128,256]{1,0:T(8,128)(2,1)} custom-call(bf16[128,128]{1,0:T(8,128)(2,1)} %refs_0_.1, bf16[128,128]{1,0:T(8,128)(2,1)} %refs_1_.1, f32[1,128]{1,0:T(1,128)} %bitcast.4, f32[1,128]{1,0:T(1,128)} %bitcast.5, f32[33,64]{1,0:T(8,128)} %refs_4_.1, f32[1,64]{1,0:T(1,128)} %bitcast.6, f32[64,64]{1,0:T(8,128)} %refs_6_.1, f32[1,64]{1,0:T(1,128)} %bitcast.7, ...), custom_call_target="tpu_custom_call" | custom-call | tf_op jit(solution)/shard_map/pallas_call | solution.py:339
  76.3 1.5 %copy.16 = bf16[128,256]{1,0:T(8,128)(2,1)} copy(bf16[128,256]{1,0:T(8,128)(2,1)} %shard_map.136) | data formatting | bytes 131072

commit v2 on v1

v2 whole, which is shorter than its diff:
```python
import functools
import math

import jax
import jax.numpy as jnp
import ml_dtypes
import numpy as np
from jax import lax
from jax.experimental import pallas as pl
from jax.experimental.pallas import tpu as pltpu
from jax.sharding import PartitionSpec as P

HIGHEST = lax.Precision.HIGHEST
F32 = jnp.float32
BF16 = jnp.bfloat16
MESH = pl.DeviceIdType.MESH


def band_frequencies(length, emb_width):
    band_count = (emb_width - 1) // 2
    return [
        min(length // 2, max(b, int((length / 2) ** ((b - 1) / (band_count - 1)))))
        for b in range(1, band_count + 1)
    ]


def two_terms(table):
    high = table.astype(np.float32).astype(ml_dtypes.bfloat16)
    low = (table - high.astype(np.float64)).astype(np.float32).astype(ml_dtypes.bfloat16)
    return high, low


def transform_tables(blocks, width):
    length = blocks * width
    k1 = np.arange(blocks)[:, None]
    b = np.arange(blocks)[None, :]
    across = 2.0 * math.pi * (k1 + 0.25) * b / blocks
    first = np.concatenate([np.cos(across), -np.sin(across)], axis=0)
    last = np.concatenate([np.cos(across).T, -np.sin(across).T], axis=1) / length
    j = np.arange(width)
    turn = 2.0 * math.pi * (k1 + 0.25) * j[None, :] / length
    twiddle = np.concatenate([np.cos(turn), np.sin(turn)]).astype(np.float32)
    within = 2.0 * math.pi * ((j[:, None] * j[None, :]) % width) / width
    cos, sin = np.cos(within), np.sin(within)
    middle = np.concatenate(two_terms(np.block([[cos, -sin], [sin, cos]])), axis=0)
    first = np.stack(
        [np.concatenate(two_terms(half) * 2, axis=1) for half in np.split(first, 2, axis=1)]
    )
    last = np.concatenate(two_terms(last), axis=1)
    return twiddle, middle, first, last


def split(value):
    high = value.astype(BF16)
    return high, (value - high.astype(F32)).astype(BF16)


def dot(left, right):
    return jnp.dot(left, right, preferred_element_type=F32)


def dot_nt(left, right):
    return lax.dot_general(left, right, (((1,), (1,)), ((), ())), preferred_element_type=F32)


def contract_first(left, right):
    return lax.dot_general(
        left, right, (((0,), (0,)), ((), ())), precision=HIGHEST, preferred_element_type=F32
    )


def hidden_block(start, length, freqs, width, w1_ref, b1_ref, w2_ref, b2_ref, pad1, pad2, hid, out):
    emb, order = w1_ref.shape
    rows = pad1.shape[0]
    row = lax.broadcasted_iota(jnp.int32, (rows, width), 0)
    time = start + lax.broadcasted_iota(jnp.int32, (rows, width), 1)
    freq = jnp.zeros((rows, width), jnp.int32)
    for band, f in enumerate(freqs):
        freq = jnp.where((row == 2 * band + 1) | (row == 2 * band + 2), f, freq)
    shift = jnp.where(lax.rem(row, 2) == 1, length // 4, 0)
    phase = lax.rem(time * freq + shift, length).astype(F32) * (2.0 * math.pi / length)
    features = jnp.where(row == 0, time.astype(F32) / length, jnp.sin(phase))
    features = jnp.where(row == emb, 1.0, jnp.where(row > emb, 0.0, features))
    pad1[...] = jnp.zeros_like(pad1)
    pad1[0:emb, :] = w1_ref[...]
    pad1[emb : emb + 1, :] = b1_ref[...]
    hid[0:order, :] = jnp.sin(contract_first(pad1[...], features))
    extra = lax.broadcasted_iota(jnp.int32, (hid.shape[0] - order, width), 0)
    hid[order:, :] = jnp.where(extra == 0, 1.0, 0.0)
    pad2[...] = jnp.zeros_like(pad2)
    pad2[0:order, :] = w2_ref[...]
    pad2[order : order + 1, :] = b2_ref[...]
    out[...] = jnp.sin(contract_first(pad2[...], hid[...]))


def filter_taps(start, length, order, params, hidden):
    rate = params[:, order : order + 1]
    shaped = jnp.dot(params[:, :order], hidden, precision=HIGHEST, preferred_element_type=F32)
    small = rate * (-2.0 / length)
    series = jnp.ones_like(small)
    for term in range(8, 1, -1):
        series = 1.0 + series * small * (1.0 / term)
    scale = lax.rsqrt((jnp.exp(-2.0 * rate) - 1.0) / (small * series))
    fraction = (start + lax.broadcasted_iota(jnp.int32, shaped.shape, 1)).astype(F32) / length
    return shaped * jnp.exp(-rate * fraction) * scale


def spectrum(blocks, halves, lhs, twiddle, middle, first):
    width = twiddle.shape[1]
    stage = None
    for which, ref in halves:
        per = ref.shape[1]
        high, low = split(jnp.concatenate([ref[:, i, :] for i in range(per)], axis=1))
        part = dot(first[which], jnp.concatenate([high, high, low, low], axis=0))
        stage = part if stage is None else stage + part
    cos, sin = twiddle[:blocks, :], twiddle[blocks:, :]
    for i in range(per):
        re = stage[:blocks, i * width : (i + 1) * width]
        im = stage[blocks:, i * width : (i + 1) * width]
        lhs[i * blocks : (i + 1) * blocks, :width] = re * cos + im * sin
        lhs[i * blocks : (i + 1) * blocks, width:] = im * cos - re * sin
    table_high, table_low = middle[: 2 * width, :], middle[2 * width :, :]
    high, low = split(lhs[...])
    return dot(high, table_high) + (dot(low, table_high) + dot(high, table_low))


def multiply(left, right):
    width = left.shape[1] // 2
    left_re, left_im, right_re, right_im = left[:, :width], left[:, width:], right[:, :width], right[:, width:]
    return jnp.concatenate(
        [left_re * right_re - left_im * right_im, left_re * right_im + left_im * right_re], axis=1
    )


def inverse(blocks, product, which, mid, twiddle, middle, last, out):
    width = twiddle.shape[1]
    table_high, table_low = middle[: 2 * width, :], middle[2 * width :, :]
    high, low = split(product)
    stage = dot_nt(high, table_high) + (dot_nt(low, table_high) + dot_nt(high, table_low))
    cos, sin = twiddle[:blocks, :], twiddle[blocks:, :]
    per = out.shape[1]
    for i in range(per):
        re = stage[i * blocks : (i + 1) * blocks, :width]
        im = stage[i * blocks : (i + 1) * blocks, width:]
        mid[:blocks, i * width : (i + 1) * width] = re * cos - im * sin
        mid[blocks:, i * width : (i + 1) * width] = re * sin + im * cos
    high, low = split(mid[...])
    table = last[which * (blocks // 2) : (which + 1) * (blocks // 2), :]
    result = dot(table, jnp.concatenate([high, high], axis=0))
    result += dot(table, jnp.concatenate([low, low], axis=0))
    for i in range(per):
        out[:, i, :] = result[:, i * width : (i + 1) * width]


def mixer_kernel(seq_size, chan_size, owners, freqs, arrays, *refs):
    sources, weight_hbm, out_ref = refs[:arrays], refs[arrays], refs[arrays + 1]
    held = refs[arrays + 2 : 2 * arrays + 2]
    x_ref, gate_ref, skip_ref, decay_ref, w1_ref, b1_ref, w2_ref, b2_ref, wl_ref = held[:9]
    twiddle, middle, first, last = held[9:]
    (
        pad1,
        pad2,
        hid,
        hidden,
        rows,
        params,
        all_params,
        send_taps,
        recv_taps,
        send_x,
        recv_x,
        lhs,
        taps_spectrum,
        product,
        mid,
        send_y,
        recv_y,
        mixed,
        gathered,
        columns,
        send_sems,
        recv_sems,
        local_sems,
    ) = refs[2 * arrays + 2 :]
    block, chans = x_ref.shape
    order = w1_ref.shape[1]
    length = seq_size * block
    half = seq_size // 2
    per = chans // owners
    share = seq_size // chan_size
    feats = out_ref.shape[1]
    d = lax.axis_index("seq")
    c = lax.axis_index("chan")
    is_owner = d < owners

    def chan_peer(k):
        return lax.rem(c + k, chan_size)

    def wait_bytes(ref, sem):
        pltpu.make_async_copy(ref, ref, sem).wait()

    def to_seq(source, target, lane, landing, p):
        pltpu.make_async_remote_copy(
            src_ref=source,
            dst_ref=target,
            send_sem=send_sems.at[lane],
            recv_sem=recv_sems.at[landing],
            device_id={"seq": p},
            device_id_type=MESH,
        ).start()

    def to_chan(source, target, lane, p):
        pltpu.make_async_remote_copy(
            src_ref=source,
            dst_ref=target,
            send_sem=send_sems.at[lane],
            recv_sem=recv_sems.at[lane],
            device_id={"chan": p},
            device_id_type=MESH,
        ).start()

    loads = [
        pltpu.make_async_copy(source, target, local_sems.at[i])
        for i, (source, target) in enumerate(zip(sources, held))
    ]
    for load in loads:
        load.start()
    barrier = pltpu.get_barrier_semaphore()

    @pl.when(is_owner)
    def _():
        @pl.loop(1, seq_size)
        def _(k):
            p = lax.rem(d + k, seq_size)
            pl.semaphore_signal(barrier, inc=1, device_id={"seq": p}, device_id_type=MESH)

    @pl.loop(1, chan_size)
    def _(k):
        pl.semaphore_signal(
            barrier, inc=1, device_id={"chan": chan_peer(k)}, device_id_type=MESH
        )

    own_columns = pltpu.make_async_copy(
        weight_hbm.at[:, pl.ds(pl.multiple_of(c * feats, feats), feats)],
        columns.at[pl.ds(pl.multiple_of(c * chans, chans), chans), :],
        local_sems.at[arrays],
    )
    own_columns.start()
    for load in loads:
        load.wait()

    send_x[...] = x_ref[...].astype(F32).T.reshape(owners, per, block)

    @pl.when(is_owner)
    def _():
        rows[...] = jnp.zeros_like(rows)
        rows[:order, :] = wl_ref[...]
        rows[order : order + 1, :] = decay_ref[...]
        params[...] = rows[...].T.reshape(owners, per, block)
        pl.semaphore_wait(barrier, owners - 1 + chan_size - 1)

    @pl.when(jnp.logical_not(is_owner))
    def _():
        pl.semaphore_wait(barrier, owners + chan_size - 1)

    @pl.loop(0, owners)
    def _(o):
        @pl.when(o != d)
        def _():
            to_seq(send_x.at[o], recv_x.at[d], 0, jnp.where(d < half, 0, 1), o)

    others = pl.ds(0, (chan_size - 1))

    @pl.when(is_owner)
    def _():
        @pl.loop(1, chan_size)
        def _(k):
            to_chan(params.at[d], all_params.at[c], 2, chan_peer(k))

        all_params[c] = params[d]
        recv_x[d] = send_x[d]
        start = c * (share * block)
        hidden_block(
            start,
            length,
            freqs,
            share * block,
            w1_ref,
            b1_ref,
            w2_ref,
            b2_ref,
            pad1,
            pad2,
            hid,
            hidden,
        )
        wait_bytes(all_params.at[others], recv_sems.at[2])
        taps = filter_taps(
            start, length, order, all_params[...].reshape(chan_size * per, block), hidden[...]
        )
        for q in range(share):
            send_taps[:, q] = taps[:, q * block : (q + 1) * block].reshape(chan_size, per, block)
        here = pl.ds(c * share, share)

        @pl.loop(1, chan_size)
        def _(k):
            p = chan_peer(k)
            to_chan(send_taps.at[p], recv_taps.at[here], 3, p)

        recv_taps[here] = send_taps[c]

    @pl.loop(1, chan_size)
    def _(k):
        p = chan_peer(k)
        to_chan(
            weight_hbm.at[:, pl.ds(pl.multiple_of(p * feats, feats), feats)],
            columns.at[pl.ds(pl.multiple_of(c * chans, chans), chans), :],
            4,
            p,
        )

    early, late = pl.ds(0, half), pl.ds(half, half)

    @pl.when(is_owner)
    def _():
        wait_bytes(recv_taps.at[pl.ds(0, (chan_size - 1) * share)], recv_sems.at[3])
        taps_spectrum[...] = spectrum(
            seq_size,
            [(0, recv_taps.at[early]), (1, recv_taps.at[late])],
            lhs,
            twiddle,
            middle,
            first,
        )
        wait_bytes(recv_x.at[pl.ds(0, half - 1)], recv_sems.at[0])
        inputs = spectrum(seq_size, [(0, recv_x.at[early])], lhs, twiddle, middle, first)
        product[...] = multiply(inputs, taps_spectrum[...])
        inverse(
            seq_size, product[...], 0, mid, twiddle, middle, last, send_y.at[early]
        )

        @pl.loop(1, half)
        def _(k):
            p = lax.rem(d + k, half)
            to_seq(send_y.at[p], recv_y.at[d], 1, 5, p)

        recv_y[d] = send_y[d]
        wait_bytes(recv_y.at[pl.ds(0, owners - 1)], recv_sems.at[5])

    @pl.when(jnp.logical_not(is_owner))
    def _():
        wait_bytes(recv_y, recv_sems.at[5])

    convolved = recv_y[...].reshape(chans, block).T
    skipped = skip_ref[...] * x_ref[...].astype(F32)
    mixed[...] = (gate_ref[...].astype(F32) * (convolved + skipped)).astype(BF16)
    place = gathered.at[:, pl.ds(pl.multiple_of(c * chans, chans), chans)]

    @pl.loop(1, chan_size)
    def _(k):
        to_chan(mixed, place, 6, chan_peer(k))

    place[...] = mixed[...]

    @pl.when(is_owner)
    def _():
        wait_bytes(recv_x.at[pl.ds(0, half)], recv_sems.at[1])
        inputs = spectrum(seq_size, [(1, recv_x.at[late])], lhs, twiddle, middle, first)
        product[...] += multiply(inputs, taps_spectrum[...])
        inverse(
            seq_size, product[...], 1, mid, twiddle, middle, last, send_y.at[late]
        )

        @pl.loop(0, half)
        def _(k):
            p = half + lax.rem(d + k, half)
            to_seq(send_y.at[p], recv_y.at[d], 1, 5, p)

    own_columns.wait()
    rest = pl.ds(0, (chan_size - 1) * chans)
    wait_bytes(columns.at[rest, :], recv_sems.at[4])
    wait_bytes(gathered.at[:, rest], recv_sems.at[6])
    out_ref[...] = dot(gathered[...], columns[...]).astype(out_ref.dtype)

    @pl.when(is_owner)
    def _():
        wait_bytes(send_x.at[pl.ds(0, owners - 1)], send_sems.at[0])
        wait_bytes(send_y.at[pl.ds(0, seq_size - 1)], send_sems.at[1])
        wait_bytes(all_params.at[others], send_sems.at[2])
        wait_bytes(send_taps.at[others], send_sems.at[3])

    @pl.when(jnp.logical_not(is_owner))
    def _():
        wait_bytes(send_x, send_sems.at[0])

    wait_bytes(columns.at[rest, :], send_sems.at[4])
    wait_bytes(gathered.at[:, rest], send_sems.at[6])


def shards(
    mixer_input,
    gate_branch,
    skip_gain,
    decay_rate,
    first_weight,
    first_bias,
    second_weight,
    second_bias,
    last_weight,
    output_weight,
):
    block, chans = mixer_input.shape
    seq_size = lax.axis_size("seq")
    chan_size = lax.axis_size("chan")
    emb, order = first_weight.shape
    feats = output_weight.shape[1] // chan_size
    owners = seq_size // 4
    per = chans // owners
    share = seq_size // chan_size
    length = block * seq_size
    held = [
        mixer_input,
        gate_branch,
        skip_gain.reshape(1, chans),
        decay_rate.reshape(1, chans),
        first_weight,
        first_bias.reshape(1, order),
        second_weight,
        second_bias.reshape(1, order),
        last_weight,
        *[jnp.asarray(table) for table in transform_tables(seq_size, block)],
    ]
    return pl.pallas_call(
        functools.partial(
            mixer_kernel, seq_size, chan_size, owners, band_frequencies(length, emb), len(held)
        ),
        out_shape=jax.ShapeDtypeStruct((block, feats), BF16),
        in_specs=[pl.BlockSpec(memory_space=pltpu.HBM)] * (len(held) + 1),
        out_specs=pl.BlockSpec(memory_space=pltpu.VMEM),
        scratch_shapes=[
            *[pltpu.VMEM(value.shape, value.dtype) for value in held],
            pltpu.VMEM((-(-(emb + 1) // 8) * 8, order), F32),
            pltpu.VMEM((order + 8, order), F32),
            pltpu.VMEM((order + 8, share * block), F32),
            pltpu.VMEM((order, share * block), F32),
            pltpu.VMEM((block, chans), F32),
            pltpu.VMEM((owners, per, block), F32),
            pltpu.VMEM((chan_size, per, block), F32),
            pltpu.VMEM((chan_size, share, per, block), F32),
            pltpu.VMEM((seq_size, per, block), F32),
            pltpu.VMEM((owners, per, block), F32),
            pltpu.VMEM((seq_size, per, block), F32),
            pltpu.VMEM((per * seq_size, 2 * block), F32),
            pltpu.VMEM((per * seq_size, 2 * block), F32),
            pltpu.VMEM((per * seq_size, 2 * block), F32),
            pltpu.VMEM((2 * seq_size, per * block), F32),
            pltpu.VMEM((seq_size, per, block), F32),
            pltpu.VMEM((owners, per, block), F32),
            pltpu.VMEM((block, chans), BF16),
            pltpu.VMEM((block, chan_size * chans), BF16),
            pltpu.VMEM((chan_size * chans, feats), BF16),
            pltpu.SemaphoreType.DMA((7,)),
            pltpu.SemaphoreType.DMA((7,)),
            pltpu.SemaphoreType.DMA((len(held) + 1,)),
        ],
        compiler_params=pltpu.CompilerParams(
            collective_id=0, has_side_effects=True, vmem_limit_bytes=62 << 20
        ),
    )(*held, output_weight)


def solution(mesh):
    in_specs = (
        P("seq", "chan"),
        P("seq", "chan"),
        P("chan"),
        P("chan"),
        P(),
        P(),
        P(),
        P(),
        P(None, "chan"),
        P("chan", None),
    )
    out_specs = P("seq", "chan")
    return jax.shard_map(shards, mesh=mesh, in_specs=in_specs, out_specs=out_specs, check_vma=False)
```

time: 78 us -> 69.2 us (0.89)
  Pallas kernels: 76.3 us -> 67.6 us
    pallas_call x1, Pallas kernels: 76.3 us -> 67.6 us  [shards(): pl.pallas_call(functools.partial(mixer_kernel, seq_size, chan_size, owner...]
where the time goes in v2:
time: 69.2 us; the launch traced here: 69.1 us
  Pallas kernels  67.6 us (98%)
  local copies, waits for them, and re-layouts  1.47 us (2%)
    pallas_call x1, Pallas kernels, shards(): pl.pallas_call(functools.partial(mixer_kernel, seq_size, chan_size, owner...  67.6 us
    unnamed x1, local copies, waits for them, and re-layouts  1.47 us

profile of v2, /device:TPU:1, one launch (start us, length us, event | category | flops | bytes accessed | tf_op | source)
XLA Modules:
  0.0 69.1 jit_solution(18369602143532487931)
XLA Ops:
  0.0 67.6 %shard_map.136 = bf16[128,256]{1,0:T(8,128)(2,1)} custom-call(bf16[128,128]{1,0:T(8,128)(2,1)} %refs_0_.1, bf16[128,128]{1,0:T(8,128)(2,1)} %refs_1_.1, f32[1,128]{1,0:T(1,128)} %bitcast.4, f32[1,128]{1,0:T(1,128)} %bitcast.5, f32[33,64]{1,0:T(8,128)} %refs_4_.1, f32[1,64]{1,0:T(1,128)} %bitcast.6, f32[64,64]{1,0:T(8,128)} %refs_6_.1, f32[1,64]{1,0:T(1,128)} %bitcast.7, ...), custom_call_target="tpu_custom_call" | custom-call | tf_op jit(solution)/shard_map/pallas_call | solution.py:433
  67.6 1.5 %copy.16 = bf16[128,256]{1,0:T(8,128)(2,1)} copy(bf16[128,256]{1,0:T(8,128)(2,1)} %shard_map.136) | data formatting | bytes 131072

commit v3 on v2

--- a/solution.py
+++ b/solution.py
@@ -102,19 +102,18 @@
         series = 1.0 + series * small * (1.0 / term)
     scale = lax.rsqrt((jnp.exp(-2.0 * rate) - 1.0) / (small * series))
     fraction = (start + lax.broadcasted_iota(jnp.int32, shaped.shape, 1)).astype(F32) / length
-    return shaped * jnp.exp(-rate * fraction) * scale
-
-
-def spectrum(blocks, halves, lhs, twiddle, middle, first):
+    skip = params[:, order + 1 : order + 2]
+    return shaped * jnp.exp(-rate * fraction) * scale + jnp.where(fraction == 0.0, skip, 0.0)
+
+
+def flat(ref):
+    return jnp.concatenate([ref[:, i, :] for i in range(ref.shape[1])], axis=1)
+
+
+def spectrum(blocks, stage, lhs, twiddle, middle):
     width = twiddle.shape[1]
-    stage = None
-    for which, ref in halves:
-        per = ref.shape[1]
-        high, low = split(jnp.concatenate([ref[:, i, :] for i in range(per)], axis=1))
-        part = dot(first[which], jnp.concatenate([high, high, low, low], axis=0))
-        stage = part if stage is None else stage + part
     cos, sin = twiddle[:blocks, :], twiddle[blocks:, :]
-    for i in range(per):
+    for i in range(stage.shape[1] // width):
         re = stage[:blocks, i * width : (i + 1) * width]
         im = stage[blocks:, i * width : (i + 1) * width]
         lhs[i * blocks : (i + 1) * blocks, :width] = re * cos + im * sin
@@ -124,6 +123,17 @@
     return dot(high, table_high) + (dot(low, table_high) + dot(high, table_low))
 
 
+def taps_stage(first, which, ref):
+    high, low = split(flat(ref))
+    return dot(first[which], jnp.concatenate([high, high, low, low], axis=0))
+
+
+def input_stage(first, which, ref, wide):
+    wide[...] = ref[...].astype(F32)
+    value = flat(wide).astype(BF16)
+    return dot(first[which, :, : 2 * value.shape[0]], jnp.concatenate([value, value], axis=0))
+
+
 def multiply(left, right):
     width = left.shape[1] // 2
     left_re, left_im, right_re, right_im = left[:, :width], left[:, width:], right[:, :width], right[:, width:]
@@ -132,7 +142,7 @@
     )
 
 
-def inverse(blocks, product, which, mid, twiddle, middle, last, out):
+def inverse(blocks, product, which, mid, twiddle, middle, last, wide, out):
     width = twiddle.shape[1]
     table_high, table_low = middle[: 2 * width, :], middle[2 * width :, :]
     high, low = split(product)
@@ -149,7 +159,8 @@
     result = dot(table, jnp.concatenate([high, high], axis=0))
     result += dot(table, jnp.concatenate([low, low], axis=0))
     for i in range(per):
-        out[:, i, :] = result[:, i * width : (i + 1) * width]
+        wide[:, i, :] = result[:, i * width : (i + 1) * width]
+    out[...] = wide[...].astype(out.dtype)
 
 
 def mixer_kernel(seq_size, chan_size, owners, freqs, arrays, *refs):
@@ -173,6 +184,7 @@
         taps_spectrum,
         product,
         mid,
+        wide,
         send_y,
         recv_y,
         mixed,
@@ -191,7 +203,9 @@
     feats = out_ref.shape[1]
     d = lax.axis_index("seq")
     c = lax.axis_index("chan")
-    is_owner = d < owners
+    base = (half - owners) // 2
+    rank = d - base
+    is_owner = (rank >= 0) & (rank < owners)
 
     def chan_peer(k):
         return lax.rem(c + k, chan_size)
@@ -249,13 +263,14 @@
     for load in loads:
         load.wait()
 
-    send_x[...] = x_ref[...].astype(F32).T.reshape(owners, per, block)
+    send_x[...] = x_ref[...].astype(F32).T.reshape(owners, per, block).astype(BF16)
 
     @pl.when(is_owner)
     def _():
         rows[...] = jnp.zeros_like(rows)
         rows[:order, :] = wl_ref[...]
         rows[order : order + 1, :] = decay_ref[...]
+        rows[order + 1 : order + 2, :] = skip_ref[...]
         params[...] = rows[...].T.reshape(owners, per, block)
         pl.semaphore_wait(barrier, owners - 1 + chan_size - 1)
 
@@ -265,9 +280,9 @@
 
     @pl.loop(0, owners)
     def _(o):
-        @pl.when(o != d)
+        @pl.when(o != rank)
         def _():
-            to_seq(send_x.at[o], recv_x.at[d], 0, jnp.where(d < half, 0, 1), o)
+            to_seq(send_x.at[o], recv_x.at[d], 0, jnp.where(d < half, 0, 1), base + o)
 
     others = pl.ds(0, (chan_size - 1))
 
@@ -275,10 +290,10 @@
     def _():
         @pl.loop(1, chan_size)
         def _(k):
-            to_chan(params.at[d], all_params.at[c], 2, chan_peer(k))
-
-        all_params[c] = params[d]
-        recv_x[d] = send_x[d]
+            to_chan(params.at[rank], all_params.at[c], 2, chan_peer(k))
+
+        all_params[c] = params[rank]
+        recv_x[d] = send_x[rank]
         start = c * (share * block)
         hidden_block(
             start,
@@ -324,36 +339,30 @@
     @pl.when(is_owner)
     def _():
         wait_bytes(recv_taps.at[pl.ds(0, (chan_size - 1) * share)], recv_sems.at[3])
-        taps_spectrum[...] = spectrum(
-            seq_size,
-            [(0, recv_taps.at[early]), (1, recv_taps.at[late])],
-            lhs,
-            twiddle,
-            middle,
-            first,
-        )
+        stage = taps_stage(first, 0, recv_taps.at[early]) + taps_stage(first, 1, recv_taps.at[late])
+        taps_spectrum[...] = spectrum(seq_size, stage, lhs, twiddle, middle)
         wait_bytes(recv_x.at[pl.ds(0, half - 1)], recv_sems.at[0])
-        inputs = spectrum(seq_size, [(0, recv_x.at[early])], lhs, twiddle, middle, first)
+        stage = input_stage(first, 0, recv_x.at[early], wide)
+        inputs = spectrum(seq_size, stage, lhs, twiddle, middle)
         product[...] = multiply(inputs, taps_spectrum[...])
         inverse(
-            seq_size, product[...], 0, mid, twiddle, middle, last, send_y.at[early]
+            seq_size, product[...], 0, mid, twiddle, middle, last, wide, send_y.at[early]
         )
 
         @pl.loop(1, half)
         def _(k):
             p = lax.rem(d + k, half)
-            to_seq(send_y.at[p], recv_y.at[d], 1, 5, p)
-
-        recv_y[d] = send_y[d]
+            to_seq(send_y.at[p], recv_y.at[rank], 1, 5, p)
+
+        recv_y[rank] = send_y[d]
         wait_bytes(recv_y.at[pl.ds(0, owners - 1)], recv_sems.at[5])
 
     @pl.when(jnp.logical_not(is_owner))
     def _():
         wait_bytes(recv_y, recv_sems.at[5])
 
-    convolved = recv_y[...].reshape(chans, block).T
-    skipped = skip_ref[...] * x_ref[...].astype(F32)
-    mixed[...] = (gate_ref[...].astype(F32) * (convolved + skipped)).astype(BF16)
+    convolved = recv_y[...].astype(F32).reshape(chans, block).T
+    mixed[...] = (gate_ref[...].astype(F32) * convolved).astype(BF16)
     place = gathered.at[:, pl.ds(pl.multiple_of(c * chans, chans), chans)]
 
     @pl.loop(1, chan_size)
@@ -365,16 +374,17 @@
     @pl.when(is_owner)
     def _():
         wait_bytes(recv_x.at[pl.ds(0, half)], recv_sems.at[1])
-        inputs = spectrum(seq_size, [(1, recv_x.at[late])], lhs, twiddle, middle, first)
+        stage = input_stage(first, 1, recv_x.at[late], wide)
+        inputs = spectrum(seq_size, stage, lhs, twiddle, middle)
         product[...] += multiply(inputs, taps_spectrum[...])
         inverse(
-            seq_size, product[...], 1, mid, twiddle, middle, last, send_y.at[late]
+            seq_size, product[...], 1, mid, twiddle, middle, last, wide, send_y.at[late]
         )
 
         @pl.loop(0, half)
         def _(k):
             p = half + lax.rem(d + k, half)
-            to_seq(send_y.at[p], recv_y.at[d], 1, 5, p)
+            to_seq(send_y.at[p], recv_y.at[rank], 1, 5, p)
 
     own_columns.wait()
     rest = pl.ds(0, (chan_size - 1) * chans)
@@ -448,14 +458,15 @@
             pltpu.VMEM((chan_size, per, block), F32),
             pltpu.VMEM((chan_size, share, per, block), F32),
             pltpu.VMEM((seq_size, per, block), F32),
-            pltpu.VMEM((owners, per, block), F32),
-            pltpu.VMEM((seq_size, per, block), F32),
+            pltpu.VMEM((owners, per, block), BF16),
+            pltpu.VMEM((seq_size, per, block), BF16),
             pltpu.VMEM((per * seq_size, 2 * block), F32),
             pltpu.VMEM((per * seq_size, 2 * block), F32),
             pltpu.VMEM((per * seq_size, 2 * block), F32),
             pltpu.VMEM((2 * seq_size, per * block), F32),
-            pltpu.VMEM((seq_size, per, block), F32),
-            pltpu.VMEM((owners, per, block), F32),
+            pltpu.VMEM((seq_size // 2, per, block), F32),
+            pltpu.VMEM((seq_size, per, block), BF16),
+            pltpu.VMEM((owners, per, block), BF16),
             pltpu.VMEM((block, chans), BF16),
             pltpu.VMEM((block, chan_size * chans), BF16),
             pltpu.VMEM((chan_size * chans, feats), BF16),

time: 69.2 us -> 59.5 us (0.86)
  the two profiles are of different devices: /device:TPU:1 before, /device:TPU:838 now
where the time goes in v3:
time: 59.5 us; the launch traced here: 59.3 us
  Pallas kernels  57.8 us (97%)
  local copies, waits for them, and re-layouts  1.47 us (2%)
    pallas_call x1, Pallas kernels, shards(): pl.pallas_call(functools.partial(mixer_kernel, seq_size, chan_size, owner...  57.8 us
    unnamed x1, local copies, waits for them, and re-layouts  1.47 us

profile of v3, /device:TPU:838, one launch (start us, length us, event | category | flops | bytes accessed | tf_op | source)
XLA Modules:
  0.0 59.3 jit_solution(6672076648511974612)
XLA Ops:
  0.0 57.8 %shard_map.136 = bf16[128,256]{1,0:T(8,128)(2,1)} custom-call(bf16[128,128]{1,0:T(8,128)(2,1)} %refs_0_.1, bf16[128,128]{1,0:T(8,128)(2,1)} %refs_1_.1, f32[1,128]{1,0:T(1,128)} %bitcast.4, f32[1,128]{1,0:T(1,128)} %bitcast.5, f32[33,64]{1,0:T(8,128)} %refs_4_.1, f32[1,64]{1,0:T(1,128)} %bitcast.6, f32[64,64]{1,0:T(8,128)} %refs_6_.1, f32[1,64]{1,0:T(1,128)} %bitcast.7, ...), custom_call_target="tpu_custom_call" | custom-call | tf_op jit(solution)/shard_map/pallas_call | solution.py:443
  57.8 1.5 %copy.16 = bf16[128,256]{1,0:T(8,128)(2,1)} copy(bf16[128,256]{1,0:T(8,128)(2,1)} %shard_map.136) | data formatting | bytes 131072

commit v4 on v3

--- a/solution.py
+++ b/solution.py
@@ -206,6 +206,9 @@
     base = (half - owners) // 2
     rank = d - base
     is_owner = (rank >= 0) & (rank < owners)
+    core = lax.rem(d, 2)
+    sibling = d + 1 - 2 * core
+    part = chans // 2
 
     def chan_peer(k):
         return lax.rem(c + k, chan_size)
@@ -248,15 +251,25 @@
             p = lax.rem(d + k, seq_size)
             pl.semaphore_signal(barrier, inc=1, device_id={"seq": p}, device_id_type=MESH)
 
+    @pl.when(jnp.logical_not(is_owner))
+    def _():
+        pl.semaphore_signal(barrier, inc=1, device_id={"seq": sibling}, device_id_type=MESH)
+
     @pl.loop(1, chan_size)
     def _(k):
         pl.semaphore_signal(
             barrier, inc=1, device_id={"chan": chan_peer(k)}, device_id_type=MESH
         )
 
+    def weight_part(p):
+        return weight_hbm.at[
+            pl.ds(pl.multiple_of(core * part, part), part),
+            pl.ds(pl.multiple_of(p * feats, feats), feats),
+        ]
+
     own_columns = pltpu.make_async_copy(
-        weight_hbm.at[:, pl.ds(pl.multiple_of(c * feats, feats), feats)],
-        columns.at[pl.ds(pl.multiple_of(c * chans, chans), chans), :],
+        weight_part(c),
+        columns.at[c, core],
         local_sems.at[arrays],
     )
     own_columns.start()
@@ -276,7 +289,7 @@
 
     @pl.when(jnp.logical_not(is_owner))
     def _():
-        pl.semaphore_wait(barrier, owners + chan_size - 1)
+        pl.semaphore_wait(barrier, owners + 1 + chan_size - 1)
 
     @pl.loop(0, owners)
     def _(o):
@@ -327,12 +340,12 @@
     @pl.loop(1, chan_size)
     def _(k):
         p = chan_peer(k)
-        to_chan(
-            weight_hbm.at[:, pl.ds(pl.multiple_of(p * feats, feats), feats)],
-            columns.at[pl.ds(pl.multiple_of(c * chans, chans), chans), :],
-            4,
-            p,
-        )
+        to_chan(weight_part(p), columns.at[c, core], 4, p)
+
+    def share_weights():
+        own_columns.wait()
+        wait_bytes(columns.at[others, 0], recv_sems.at[4])
+        to_seq(columns.at[:, core], columns.at[:, core], 5, 7, sibling)
 
     early, late = pl.ds(0, half), pl.ds(half, half)
 
@@ -359,6 +372,7 @@
 
     @pl.when(jnp.logical_not(is_owner))
     def _():
+        share_weights()
         wait_bytes(recv_y, recv_sems.at[5])
 
     convolved = recv_y[...].astype(F32).reshape(chans, block).T
@@ -373,6 +387,7 @@
 
     @pl.when(is_owner)
     def _():
+        share_weights()
         wait_bytes(recv_x.at[pl.ds(0, half)], recv_sems.at[1])
         stage = input_stage(first, 1, recv_x.at[late], wide)
         inputs = spectrum(seq_size, stage, lhs, twiddle, middle)
@@ -386,11 +401,11 @@
             p = half + lax.rem(d + k, half)
             to_seq(send_y.at[p], recv_y.at[rank], 1, 5, p)
 
-    own_columns.wait()
     rest = pl.ds(0, (chan_size - 1) * chans)
-    wait_bytes(columns.at[rest, :], recv_sems.at[4])
+    wait_bytes(columns.at[:, 0], recv_sems.at[7])
     wait_bytes(gathered.at[:, rest], recv_sems.at[6])
-    out_ref[...] = dot(gathered[...], columns[...]).astype(out_ref.dtype)
+    weights = columns[...].reshape(chan_size * chans, feats)
+    out_ref[...] = dot(gathered[...], weights).astype(out_ref.dtype)
 
     @pl.when(is_owner)
     def _():
@@ -403,7 +418,8 @@
     def _():
         wait_bytes(send_x, send_sems.at[0])
 
-    wait_bytes(columns.at[rest, :], send_sems.at[4])
+    wait_bytes(columns.at[others, 0], send_sems.at[4])
+    wait_bytes(columns.at[:, 0], send_sems.at[5])
     wait_bytes(gathered.at[:, rest], send_sems.at[6])
 
 
@@ -469,9 +485,9 @@
             pltpu.VMEM((owners, per, block), BF16),
             pltpu.VMEM((block, chans), BF16),
             pltpu.VMEM((block, chan_size * chans), BF16),
-            pltpu.VMEM((chan_size * chans, feats), BF16),
+            pltpu.VMEM((chan_size, 2, chans // 2, feats), BF16),
             pltpu.SemaphoreType.DMA((7,)),
-            pltpu.SemaphoreType.DMA((7,)),
+            pltpu.SemaphoreType.DMA((8,)),
             pltpu.SemaphoreType.DMA((len(held) + 1,)),
         ],
         compiler_params=pltpu.CompilerParams(

time: 59.5 us -> 55.3 us (0.929)
  the two profiles are of different devices: /device:TPU:838 before, /device:TPU:833 now
where the time goes in v4:
time: 55.3 us; the launch traced here: 55.1 us
  Pallas kernels  53.6 us (97%)
  local copies, waits for them, and re-layouts  1.47 us (3%)
    pallas_call x1, Pallas kernels, shards(): pl.pallas_call(functools.partial(mixer_kernel, seq_size, chan_size, owner...  53.6 us
    unnamed x1, local copies, waits for them, and re-layouts  1.47 us

profile of v4, /device:TPU:833, one launch (start us, length us, event | category | flops | bytes accessed | tf_op | source)
XLA Modules:
  0.0 55.1 jit_solution(15359874631472405885)
XLA Ops:
  0.0 53.6 %shard_map.136 = bf16[128,256]{1,0:T(8,128)(2,1)} custom-call(bf16[128,128]{1,0:T(8,128)(2,1)} %refs_0_.1, bf16[128,128]{1,0:T(8,128)(2,1)} %refs_1_.1, f32[1,128]{1,0:T(1,128)} %bitcast.4, f32[1,128]{1,0:T(1,128)} %bitcast.5, f32[33,64]{1,0:T(8,128)} %refs_4_.1, f32[1,64]{1,0:T(1,128)} %bitcast.6, f32[64,64]{1,0:T(8,128)} %refs_6_.1, f32[1,64]{1,0:T(1,128)} %bitcast.7, ...), custom_call_target="tpu_custom_call" | custom-call | tf_op jit(solution)/shard_map/pallas_call | solution.py:459
  53.6 1.5 %copy.16 = bf16[128,256]{1,0:T(8,128)(2,1)} copy(bf16[128,256]{1,0:T(8,128)(2,1)} %shard_map.136) | data formatting | bytes 131072

commit v5 on v4

--- a/solution.py
+++ b/solution.py
@@ -337,10 +337,11 @@
 
         recv_taps[here] = send_taps[c]
 
-    @pl.loop(1, chan_size)
-    def _(k):
-        p = chan_peer(k)
-        to_chan(weight_part(p), columns.at[c, core], 4, p)
+    def send_weights():
+        @pl.loop(1, chan_size)
+        def _(k):
+            p = chan_peer(k)
+            to_chan(weight_part(p), columns.at[c, core], 4, p)
 
     def share_weights():
         own_columns.wait()
@@ -368,10 +369,12 @@
             to_seq(send_y.at[p], recv_y.at[rank], 1, 5, p)
 
         recv_y[rank] = send_y[d]
+        send_weights()
         wait_bytes(recv_y.at[pl.ds(0, owners - 1)], recv_sems.at[5])
 
     @pl.when(jnp.logical_not(is_owner))
     def _():
+        send_weights()
         share_weights()
         wait_bytes(recv_y, recv_sems.at[5])
 

time: 55.3 us -> 53.4 us (0.966)
  the two profiles are of different devices: /device:TPU:833 before, /device:TPU:832 now
where the time goes in v5:
time: 53.4 us; the launch traced here: 53.2 us
  Pallas kernels  51.7 us (97%)
  local copies, waits for them, and re-layouts  1.47 us (3%)
    pallas_call x1, Pallas kernels, shards(): pl.pallas_call(functools.partial(mixer_kernel, seq_size, chan_size, owner...  51.7 us
    unnamed x1, local copies, waits for them, and re-layouts  1.47 us

profile of v5, /device:TPU:832, one launch (start us, length us, event | category | flops | bytes accessed | tf_op | source)
XLA Modules:
  0.0 53.2 jit_solution(11571348278497913539)
XLA Ops:
  0.0 51.7 %shard_map.136 = bf16[128,256]{1,0:T(8,128)(2,1)} custom-call(bf16[128,128]{1,0:T(8,128)(2,1)} %refs_0_.1, bf16[128,128]{1,0:T(8,128)(2,1)} %refs_1_.1, f32[1,128]{1,0:T(1,128)} %bitcast.4, f32[1,128]{1,0:T(1,128)} %bitcast.5, f32[33,64]{1,0:T(8,128)} %refs_4_.1, f32[1,64]{1,0:T(1,128)} %bitcast.6, f32[64,64]{1,0:T(8,128)} %refs_6_.1, f32[1,64]{1,0:T(1,128)} %bitcast.7, ...), custom_call_target="tpu_custom_call" | custom-call | tf_op jit(solution)/shard_map/pallas_call | solution.py:462
  51.7 1.5 %copy.16 = bf16[128,256]{1,0:T(8,128)(2,1)} copy(bf16[128,256]{1,0:T(8,128)(2,1)} %shard_map.136) | data formatting | bytes 131072
